TPU v7x, 32 devices: a whole 2x2x4 slice. The times are simulated.
32 devices in a mesh: fsdp: 4 (over z), replica: 2 (over x), tensor: 4 (over y, core).
Axes of the slice: x: 2, y: 2, z: 4, core: 2. Of those that a mesh axis runs over, the one named last changes fastest.
Arguments:
- tokens: bfloat16 [1024, 8192], P(('fsdp', 'replica')), may hold values from -6 to 6
- weight_codes: bfloat16 [8192, 14336], P('fsdp', 'tensor'), may hold values from -127 to 127, as said below
- scales: float32 [64, 14336], P('fsdp', 'tensor'), may hold values from 3e-05 to 0.0003
- cotangent: bfloat16 [1024, 14336], P(('fsdp', 'replica'), 'tensor'), may hold values from -6 to 6
- sign_bits: int32 [14336], P('tensor'), may hold values from 0 to 1
Outputs:
- activation: bfloat16 [1024, 14336], P(('fsdp', 'replica'), 'tensor')
- input_grad: bfloat16 [1024, 8192], P(('fsdp', 'replica'), 'tensor')
- grad_codes: float32 [8192, 14336], P(('fsdp', 'replica'), 'tensor')
Inputs may be any that keep to these rules, and one draw needn't show every extreme that they name: `weight_codes`: integer values, held exactly.
All inputs are finite; a program needn't handle non-finite values.
Results may differ from a plain program's by a relative error of at most 0.015.
Values may be sent and summed in bfloat16 or wider, within the bound.
A program may use at most 128 MiB of HBM per device.

v0:
```python
import jax
import jax.numpy as jnp
from jax import lax
from jax.sharding import PartitionSpec as P

HB = 128


def hadamard_table(length):
    indices = jnp.arange(length, dtype=jnp.int32)
    intersection_bits = jnp.bitwise_and(indices[:, None], indices[None, :])
    parity = jnp.zeros((length, length), jnp.int32)
    for bit_pos in range(length.bit_length() - 1):
        parity = parity + jnp.bitwise_and(jnp.right_shift(intersection_bits, bit_pos), 1)
    return (1 - 2 * (parity % 2)).astype(jnp.float32)


def rotate_blocks(matrix, sign_bits, scaling):
    height, width = matrix.shape
    signed = matrix * (2 * sign_bits - 1).astype(jnp.float32)[None, :]
    blocks = signed.reshape(height, width // HB, HB)
    turned = jnp.einsum("rbi,ij->rbj", blocks, hadamard_table(HB), precision=lax.Precision.HIGHEST)
    return turned.reshape(height, width) * scaling


def shards(tokens, weight_codes, scales, cotangent, sign_bits):
    local_tokens = tokens.shape[0]
    shard_rows, hidden_cols = weight_codes.shape
    block_rows = shard_rows // scales.shape[0]
    weight = (
        (
            weight_codes.astype(jnp.float32).reshape(scales.shape[0], block_rows, hidden_cols)
            * scales[:, None, :]
        )
        .reshape(shard_rows, hidden_cols)
        .astype(jnp.bfloat16)
    )
    columns = lax.all_to_all(tokens, "fsdp", split_axis=1, concat_axis=0, tiled=True)
    token_rows = columns
    hidden = lax.psum_scatter(
        jnp.dot(token_rows, weight, preferred_element_type=jnp.float32).astype(jnp.bfloat16),
        "fsdp",
        scatter_dimension=0,
        tiled=True,
    ).astype(jnp.float32)
    sigmoid_val = jax.nn.sigmoid(hidden)
    activation = (hidden * sigmoid_val).astype(jnp.bfloat16)
    hidden_grad = (
        cotangent.astype(jnp.float32) * sigmoid_val * (1.0 + hidden * (1.0 - sigmoid_val))
    ).astype(jnp.bfloat16)
    arrived = lax.all_gather(hidden_grad, "fsdp", axis=0, tiled=True)
    token_rows = columns
    weight_grad = lax.dot_general(
        token_rows, arrived, (((0,), (0,)), ((), ())), preferred_element_type=jnp.float32
    )
    product = lax.dot_general(
        arrived, weight, (((1,), (1,)), ((), ())), preferred_element_type=jnp.float32
    ).astype(jnp.bfloat16)
    input_rows = product
    weight_grad, input_rows = (weight_grad, input_rows)
    returned = lax.all_to_all(input_rows, "fsdp", split_axis=0, concat_axis=1, tiled=True)
    input_grad = lax.psum_scatter(
        returned.astype(jnp.float32).astype(jnp.bfloat16), "tensor", scatter_dimension=1, tiled=True
    )
    total_tokens = local_tokens * lax.axis_size("fsdp") * lax.axis_size("replica")
    scaling = 1.0 / jnp.sqrt(jnp.float32(HB) * jnp.float32(total_tokens))
    grad_codes = rotate_blocks(
        lax.psum_scatter(
            weight_grad.astype(jnp.bfloat16), "replica", scatter_dimension=0, tiled=True
        ).astype(jnp.float32),
        sign_bits,
        scaling,
    )
    return (activation, input_grad, grad_codes)


def solution(mesh):
    return jax.shard_map(
        shards,
        mesh=mesh,
        in_specs=(
            P(("fsdp", "replica"), None),
            P("fsdp", "tensor"),
            P("fsdp", "tensor"),
            P(("fsdp", "replica"), "tensor"),
            P("tensor"),
        ),
        out_specs=(
            P(("fsdp", "replica"), "tensor"),
            P(("fsdp", "replica"), "tensor"),
            P(("fsdp", "replica"), "tensor"),
        ),
        check_vma=False,
    )
```

profile of v0, /device:TPU:0, one launch (start us, length us, event | category | flops | bytes accessed | tf_op | source)
XLA Modules:
  0.0 463.2 jit_solution(12384013270102566466)
XLA Ops:
  7.2 0.0 copy-start.1
  7.2 4.1 copy.25
  11.3 6.3 %all-to-all-start = ((bf16[128,4,2048]{0,2,1:T(8,128)(2,1)}), bf16[128,4,2048]{0,2,1:T(8,128)(2,1)S(1)}, u32[]{:S(2)}, u32[]{:S(2)}) async-start(bf16[128,4,2048]{0,2,1:T(8,128)(2,1)} %bitcast.32), calls=%async_computation | async-start | bytes 4194304 | tf_op jit(solution)/shard_map/all_to_all | solution.py:38
  17.6 0.0 reduce-scatter.10.cloned.1.call-start
  17.6 0.0 copy-done.1
  17.6 14.0 %fusion = bf16[2048,3584]{1,0:T(8,128)(2,1)} fusion(bf16[2048,3584]{1,0:T(8,128)(2,1)} %param.6, f32[16,3584]{1,0:T(8,128)S(1)} %copy-done.1), kind=kLoop, calls=%fused_computation.1 | loop fusion | flops 22020096 | bytes 29589504 | tf_op jit(solution)/shard_map/convert_element_type | solution.py:36
  31.7 34.2 %all-to-all-done = bf16[128,4,2048]{0,2,1:T(8,128)(2,1)S(1)} async-done(((bf16[128,4,2048]{0,2,1:T(8,128)(2,1)}), bf16[128,4,2048]{0,2,1:T(8,128)(2,1)S(1)}, u32[]{:S(2)}, u32[]{:S(2)}) %all-to-all-start) | async-done | bytes 2097184 | tf_op jit(solution)/shard_map/all_to_all | solution.py:38
  65.8 2.7 copy.26
  68.5 13.0 %fusion.2 = bf16[512,3584]{0,1:T(8,128)(2,1)} fusion(bf16[2048,3584]{1,0:T(8,128)(2,1)} %fusion, bf16[512,2048]{1,0:T(8,128)(2,1)} %bitcast.34), kind=kOutput, calls=%fused_computation.7 | convolution fusion | flops 7518027776 | bytes 20447232 | tf_op jit(solution)/shard_map/dot_general | solution.py:41
  81.5 6.0 %copy.33 = bf16[512,3584]{1,0:T(8,128)(2,1)} copy(bf16[512,3584]{0,1:T(8,128)(2,1)} %fusion.2) | data formatting | bytes 7340032
  87.5 0.0 copy-start
  87.5 0.0 reduce-scatter.10.cloned.1.call-update
  87.5 0.0 all-gather.2.cloned.1.call-start
  87.6 1.1 copy-done
  88.7 0.6 copy.27
  89.3 66.1 %reduce-scatter.10.cloned.1.call-done = bf16[128,3584]{1,0:T(8,128)(2,1)} async-done(((bf16[512,3584]{1,0:T(8,128)(2,1)}), bf16[128,3584]{1,0:T(8,128)(2,1)}) %reduce-scatter.10.cloned.1.call-update) | async-done | bytes 917520
  155.4 1.5 copy.34
  156.9 1.8 fusion.9
  158.7 0.0 all-gather.2.cloned.1.call-update
  158.7 0.0 reduce-scatter.8.cloned.1.call-start
  158.8 72.3 %all-gather.2.cloned.1.call-done = bf16[512,3584]{0,1:T(8,128)(2,1)} async-done(((bf16[128,3584]{0,1:T(8,128)(2,1)}), bf16[512,3584]{0,1:T(8,128)(2,1)}) %all-gather.2.cloned.1.call-update) | async-done | bytes 3670032 | tf_op jit(solution)/shard_map/all_gather | solution.py:51
  231.1 13.1 %fusion.1 = bf16[2048,3584]{0,1:T(8,128)(2,1)} fusion(bf16[512,3584]{0,1:T(8,128)(2,1)} %all-gather.2.cloned.1.call-done, bf16[512,2048]{1,0:T(8,128)(2,1)} %bitcast.35), kind=kOutput, calls=%fused_computation.4 | convolution fusion | flops 7523532800 | bytes 20447232 | tf_op jit(solution)/shard_map/dot_general | solution.py:53
  244.2 0.0 reduce-scatter.8.cloned.1.call-update
  244.3 0.2 reduce-scatter.6.cloned.1.call-start
  244.5 12.3 %convolution_convert_fusion.2 = bf16[512,2048]{1,0:T(8,128)(2,1)S(1)} fusion(bf16[512,3584]{0,1:T(8,128)(2,1)} %all-gather.2.cloned.1.call-done, bf16[2048,3584]{1,0:T(8,128)(2,1)} %fusion), kind=kOutput, calls=%fused_computation.8 | convolution fusion | flops 7517241344 | bytes 20447232 | tf_op jit(solution)/shard_map/dot_general | solution.py:56
  256.8 50.6 %all_to_all.38 = bf16[4,128,2048]{2,1,0:T(8,128)(2,1)S(1)} all-to-all(bf16[4,128,2048]{2,1,0:T(8,128)(2,1)S(1)} %bitcast.36), channel_id=1, replica_groups=mesh['fsdp'=4,'replica'=2,'tensor'=4] {'fsdp'}, dimensions={0} | all-to-all | bytes 4194304 | tf_op jit(solution)/shard_map/all_to_all | solution.py:61
  307.5 0.0 copy-start.2
  307.5 1.5 copy.35
  308.9 0.0 reduce-scatter.6.cloned.1.call-update
  309.0 0.0 copy-done.2
  309.0 1.3 copy.30
  310.3 99.5 %reduce-scatter.8.cloned.1.call-done = bf16[1024,3584]{0,1:T(8,128)(2,1)} async-done(((bf16[2048,3584]{0,1:T(8,128)(2,1)}), bf16[1024,3584]{0,1:T(8,128)(2,1)}) %reduce-scatter.8.cloned.1.call-update) | async-done | bytes 7340048 | tf_op jit(solution)/shard_map/reduce_scatter | solution.py:68
  409.7 9.6 %convert_multiply_fusion = f32[1024,3584]{0,1:T(8,128)} fusion(bf16[1024,3584]{0,1:T(8,128)(2,1)} %reduce-scatter.8.cloned.1.call-done, f32[3584]{0:T(1024)S(1)} %add_convert_fusion), kind=kLoop, calls=%fused_computation.3 | loop fusion | flops 7340032 | bytes 22034432 | tf_op jit(solution)/shard_map/mul | solution.py:20
  419.3 23.1 %convolution_multiply_fusion = f32[1024,28,128]{0,2,1:T(8,128)} fusion(f32[1024,28,128]{0,2,1:T(8,128)} %bitcast.29), kind=kOutput, calls=%fused_computation.5 | convolution fusion | flops 5641388032 | bytes 29360128 | tf_op jit(solution)/shard_map/rbi,ij->rbj/dot_general | solution.py:22
  442.4 14.3 %copy.31 = f32[1024,3584]{1,0:T(8,128)} copy(f32[1024,3584]{0,1:T(8,128)} %bitcast.28) | data formatting | bytes 29360128
  456.6 0.0 reduce-scatter.6.cloned.1.call-done
  (1 shorter events, 0.0 us)
Async XLA Ops:
  7.2 10.5 %copy-start.1 = (f32[16,3584]{1,0:T(8,128)S(1)}, f32[16,3584]{1,0:T(8,128)}, u32[]{:S(2)}) copy-start(f32[16,3584]{1,0:T(8,128)} %param.7) | copy-start | bytes 688132
  11.3 54.5 %all-to-all-start = ((bf16[128,4,2048]{0,2,1:T(8,128)(2,1)}), bf16[128,4,2048]{0,2,1:T(8,128)(2,1)S(1)}, u32[]{:S(2)}, u32[]{:S(2)}) async-start(bf16[128,4,2048]{0,2,1:T(8,128)(2,1)} %bitcast.32), calls=%async_computation | async-start | bytes 4194304 | tf_op jit(solution)/shard_map/all_to_all | solution.py:38
  17.6 137.7 %reduce-scatter.10.cloned.1.call-start = ((), (), s32[]{:S(2)}) async-start(), calls=%async_computation.8 | async-start | bytes 4587520
  87.5 1.2 copy-start
  87.5 143.6 %all-gather.2.cloned.1.call-start = ((), (), s32[]{:S(2)}) async-start(), calls=%async_computation.5 | async-start | bytes 4587520 | tf_op jit(solution)/shard_map/all_gather | solution.py:51
  158.7 251.0 %reduce-scatter.8.cloned.1.call-start = ((), (), s32[]{:S(2)}) async-start(), calls=%async_computation.7 | async-start | bytes 22020096 | tf_op jit(solution)/shard_map/reduce_scatter | solution.py:68
  244.3 212.4 %reduce-scatter.6.cloned.1.call-start = ((), (), s32[]{:S(2)}) async-start(), calls=%async_computation.6 | async-start | bytes 2621440 | tf_op jit(solution)/shard_map/reduce_scatter | solution.py:62
  307.5 1.5 copy-start.2
Sparse Core Ops, SparseCore 0:
  87.7 67.6 reduce-scatter.9
  158.9 72.1 all-gather.1
  244.4 165.3 reduce-scatter.7
  412.7 31.1 reduce-scatter.5
where the time goes:
time: 464 us; the launch traced here: 463 us
  waiting for transfers between devices  272 us (59%)
  matrix products  61.6 us (13%)
  blocking collectives  50.6 us (11%)
  local copies, waits for them, and re-layouts  33 us (7%)
  other arithmetic  25.4 us (5%)
  between operations  13.8 us (3%)
  starting transfers between devices  6.65 us (1%)
    reduce_scatter x1, waiting for transfers between devices, shards(): lax.psum_scatter(weight_grad.astype(jnp.bfloat16), 'replica', scatter_dim...  99.5 us
    all_gather x1, waiting for transfers between devices, shards(): arrived = lax.all_gather(hidden_grad, 'fsdp', axis=0, tiled=True)  72.3 us
    unnamed x5, waiting for transfers between devices  66.1 us
    all_to_all x1, blocking collectives, shards(): lax.all_to_all(input_rows, 'fsdp', split_axis=0, concat_axis=1, tiled=True)  50.6 us
    all_to_all x1, waiting for transfers between devices, shards(): lax.all_to_all(tokens, 'fsdp', split_axis=1, concat_axis=0, tiled=True)  34.2 us
    unnamed x12, local copies, waits for them, and re-layouts  28.9 us
    dot_general x1, matrix products, rotate_blocks(): jnp.einsum('rbi,ij->rbj', blocks, hadamard_table(HB), precision=lax.Preci...  23.1 us
    convert_element_type x1, other arithmetic, shards(): weight = (weight_codes.astype(jnp.float32).reshape(scales.shape[0], block...  14 us
  transfers between devices with their start and end apart: 5, of which 4 were waited for; matrix products, arithmetic and copies ran while one was open for 17% of the time, Pallas kernels for 0%

commit v1 on v0

--- a/solution.py
+++ b/solution.py
@@ -1,9 +1,27 @@
+import functools
 import jax
 import jax.numpy as jnp
 from jax import lax
 from jax.sharding import PartitionSpec as P
+from jax.lax import axis_index, ppermute, psum
 
 HB = 128
+
+
+def recast_chunk_here(my_tile, link_axis):
+    n = psum(1, axis_name=link_axis)
+    buffer = [(j0, (j0 + 1) % n) for j0 in range(n)]
+
+    def _wrap_tables(back):
+        if len(back) == n:
+            return back
+        return _wrap_tables([ppermute(back[0], link_axis, perm=buffer), *back])
+
+    everything = jnp.concatenate(_wrap_tables([my_tile]), axis=0)
+    return jnp.roll(everything, shift=(axis_index(link_axis) + 1) * my_tile.shape[0], axis=0)
+
+
+_reach_rates = functools.partial(recast_chunk_here, link_axis="fsdp")
 
 
 def hadamard_table(length):
@@ -48,7 +66,7 @@
     hidden_grad = (
         cotangent.astype(jnp.float32) * sigmoid_val * (1.0 + hidden * (1.0 - sigmoid_val))
     ).astype(jnp.bfloat16)
-    arrived = lax.all_gather(hidden_grad, "fsdp", axis=0, tiled=True)
+    arrived = _reach_rates(hidden_grad)
     token_rows = columns
     weight_grad = lax.dot_general(
         token_rows, arrived, (((0,), (0,)), ((), ())), preferred_element_type=jnp.float32

time: 464 us -> 469 us (1.011)
  local copies, waits for them, and re-layouts: 33 us -> 42.9 us
    all_gather x1 -> x0, waiting for transfers between devices: 72.3 us -> none  [shards(): arrived = lax.all_gather(hidden_grad, 'fsdp', axis=0, tiled=True)]
    ppermute x0 -> x3, waiting for transfers between devices: none -> 67.1 us  [_wrap_tables(): return _wrap_tables([ppermute(back[0], link_axis, perm=buffer), *back])]
    unnamed x12 -> x23, local copies, waits for them, and re-layouts: 28.9 us -> 38.4 us
    unnamed x5 -> x4, waiting for transfers between devices: 66.1 us -> 67.2 us
  transfers between devices with their start and end apart: 5 -> 7, of which waited for: 4 -> 6; matrix products, arithmetic and copies ran while one was open for 17% -> 16% of each run, Pallas kernels for 0% -> 0%
where the time goes in v1:
time: 469 us; the launch traced here: 468 us
  waiting for transfers between devices  271 us (58%)
  matrix products  59.5 us (13%)
  blocking collectives  48 us (10%)
  local copies, waits for them, and re-layouts  42.9 us (9%)
  other arithmetic  25.6 us (5%)
  between operations  13.9 us (3%)
  starting transfers between devices  7.74 us (2%)
    reduce_scatter x1, waiting for transfers between devices, shards(): lax.psum_scatter(weight_grad.astype(jnp.bfloat16), 'replica', scatter_dim...  102 us
    unnamed x4, waiting for transfers between devices  67.2 us
    ppermute x3, waiting for transfers between devices, _wrap_tables(): return _wrap_tables([ppermute(back[0], link_axis, perm=buffer), *back])  67.1 us
    all_to_all x1, blocking collectives, shards(): lax.all_to_all(input_rows, 'fsdp', split_axis=0, concat_axis=1, tiled=True)  48 us
    unnamed x23, local copies, waits for them, and re-layouts  38.4 us
    all_to_all x1, waiting for transfers between devices, shards(): lax.all_to_all(tokens, 'fsdp', split_axis=1, concat_axis=0, tiled=True)  34.2 us
    dot_general x1, matrix products, rotate_blocks(): jnp.einsum('rbi,ij->rbj', blocks, hadamard_table(HB), precision=lax.Preci...  23.1 us
    convert_element_type x1, other arithmetic, shards(): weight = (weight_codes.astype(jnp.float32).reshape(scales.shape[0], block...  14 us
  transfers between devices with their start and end apart: 7, of which 6 were waited for; matrix products, arithmetic and copies ran while one was open for 16% of the time, Pallas kernels for 0%

profile of v1, /device:TPU:0, one launch (start us, length us, event | category | flops | bytes accessed | tf_op | source)
XLA Modules:
  0.0 468.3 jit_solution(3512316599479265190)
XLA Ops:
  7.2 0.0 copy-start.2
  7.2 4.1 copy.25
  11.3 6.3 %all-to-all-start = ((bf16[128,4,2048]{0,2,1:T(8,128)(2,1)}), bf16[128,4,2048]{0,2,1:T(8,128)(2,1)S(1)}, u32[]{:S(2)}, u32[]{:S(2)}) async-start(bf16[128,4,2048]{0,2,1:T(8,128)(2,1)} %bitcast.30), calls=%async_computation | async-start | bytes 4194304 | tf_op jit(solution)/shard_map/all_to_all | solution.py:56
  17.6 0.0 reduce-scatter.10.cloned.1.call-start
  17.6 0.0 copy-done.2
  17.6 14.0 %fusion = bf16[2048,3584]{1,0:T(8,128)(2,1)} fusion(bf16[2048,3584]{1,0:T(8,128)(2,1)} %param.6, f32[16,3584]{1,0:T(8,128)S(1)} %copy-done.2), kind=kLoop, calls=%fused_computation.1 | loop fusion | flops 22020096 | bytes 29589504 | tf_op jit(solution)/shard_map/convert_element_type | solution.py:54
  31.7 34.2 %all-to-all-done = bf16[128,4,2048]{0,2,1:T(8,128)(2,1)S(1)} async-done(((bf16[128,4,2048]{0,2,1:T(8,128)(2,1)}), bf16[128,4,2048]{0,2,1:T(8,128)(2,1)S(1)}, u32[]{:S(2)}, u32[]{:S(2)}) %all-to-all-start) | async-done | bytes 2097184 | tf_op jit(solution)/shard_map/all_to_all | solution.py:56
  65.8 2.7 copy.26
  68.5 13.1 %fusion.2 = bf16[512,3584]{0,1:T(8,128)(2,1)} fusion(bf16[2048,3584]{1,0:T(8,128)(2,1)} %fusion, bf16[512,2048]{1,0:T(8,128)(2,1)} %bitcast.32), kind=kOutput, calls=%fused_computation.7 | convolution fusion | flops 7518027776 | bytes 20447232 | tf_op jit(solution)/shard_map/dot_general | solution.py:59
  81.6 0.0 copy-start.1
  81.6 6.1 %copy.33 = bf16[512,3584]{1,0:T(8,128)(2,1)} copy(bf16[512,3584]{0,1:T(8,128)(2,1)} %fusion.2) | data formatting | bytes 7340032
  87.7 0.0 reduce-scatter.10.cloned.1.call-update
  87.7 0.0 reduce-scatter.8.cloned.1.call-start
  87.7 0.0 copy-done.1
  87.7 0.6 copy.27
  88.4 67.1 %reduce-scatter.10.cloned.1.call-done = bf16[128,3584]{1,0:T(8,128)(2,1)} async-done(((bf16[512,3584]{1,0:T(8,128)(2,1)}), bf16[128,3584]{1,0:T(8,128)(2,1)}) %reduce-scatter.10.cloned.1.call-update) | async-done | bytes 917520
  155.5 2.2 copy.34
  157.7 2.0 fusion.15
  159.7 1.3 collective-permute-start
  161.0 22.3 %collective-permute-done = bf16[128,3584]{0,1:T(8,128)(2,1)S(1)} collective-permute-done((bf16[128,3584]{0,1:T(8,128)(2,1)S(1)}, bf16[128,3584]{0,1:T(8,128)(2,1)S(1)}, u32[]{:S(2)}, u32[]{:S(2)}) %collective-permute-start) | collective-permute-done | bytes 917536 | tf_op jit(solution)/shard_map/ppermute | solution.py:18
  183.3 0.0 collective-permute-start.1
  183.3 22.8 %collective-permute-done.1 = bf16[128,3584]{0,1:T(8,128)(2,1)} collective-permute-done((bf16[128,3584]{0,1:T(8,128)(2,1)S(1)}, bf16[128,3584]{0,1:T(8,128)(2,1)}, u32[]{:S(2)}, u32[]{:S(2)}) %collective-permute-start.1) | collective-permute-done | bytes 917536 | tf_op jit(solution)/shard_map/ppermute | solution.py:18
  206.1 0.0 collective-permute-start.2
  206.1 0.0 copy-start
  206.1 22.1 %collective-permute-done.2 = bf16[128,3584]{0,1:T(8,128)(2,1)} collective-permute-done((bf16[128,3584]{0,1:T(8,128)(2,1)}, bf16[128,3584]{0,1:T(8,128)(2,1)}, u32[]{:S(2)}, u32[]{:S(2)}) %collective-permute-start.2) | collective-permute-done | bytes 917536 | tf_op jit(solution)/shard_map/ppermute | solution.py:18
  228.2 1.4 constant_dynamic-update-slice_fusion.7
  229.6 1.5 constant_dynamic-update-slice_fusion.6
  231.1 0.3 constant_dynamic-update-slice_fusion.5
  231.4 0.3 constant_dynamic-update-slice_fusion.4
  231.8 1.5 constant_dynamic-update-slice_fusion.3
  233.3 1.5 constant_dynamic-update-slice_fusion.2
  234.8 0.3 constant_dynamic-update-slice_fusion.1
  235.1 0.3 constant_dynamic-update-slice_fusion
  235.4 0.0 copy-start.3
  235.4 3.0 copy-done.3
  238.4 0.0 copy-done
  238.4 11.0 %fusion.1 = bf16[2048,3584]{0,1:T(8,128)(2,1)} fusion(bf16[512,2048]{1,0:T(8,128)(2,1)S(1)} %bitcast.33, bf16[1024,3584]{0,1:T(8,128)(2,1)S(1)} %constant_dynamic-update-slice_fusion, s32[]{:T(128)S(6)} %select_n.20), kind=kOutput, calls=%fused_computation.4 | convolution fusion | flops 7523532800 | bytes 20447236 | tf_op jit(solution)/shard_map/dot_general | solution.py:71
  249.4 0.0 reduce-scatter.8.cloned.1.call-update
  249.4 0.0 reduce-scatter.6.cloned.1.call-start
  249.5 12.3 %fusion.6 = bf16[512,2048]{1,0:T(8,128)(2,1)S(1)} fusion(bf16[2048,3584]{1,0:T(8,128)(2,1)} %fusion, bf16[1024,3584]{0,1:T(8,128)(2,1)} %copy-done.3, s32[]{:T(128)S(6)} %select_n.20), kind=kOutput, calls=%fused_computation.11 | convolution fusion | flops 7517241344 | bytes 20447236 | tf_op jit(solution)/shard_map/dot_general | solution.py:74
  261.8 0.0 copy-start.4
  261.8 48.0 %all_to_all.38 = bf16[4,128,2048]{2,1,0:T(8,128)(2,1)S(1)} all-to-all(bf16[4,128,2048]{2,1,0:T(8,128)(2,1)S(1)} %bitcast.34), channel_id=1, replica_groups=mesh['fsdp'=4,'replica'=2,'tensor'=4] {'fsdp'}, dimensions={0} | all-to-all | bytes 4194304 | tf_op jit(solution)/shard_map/all_to_all | solution.py:79
  309.8 1.5 copy.35
  311.3 0.0 reduce-scatter.6.cloned.1.call-update
  311.3 0.0 copy-done.4
  311.3 1.3 copy.30
  312.6 102.2 %reduce-scatter.8.cloned.1.call-done = bf16[1024,3584]{0,1:T(8,128)(2,1)} async-done(((bf16[2048,3584]{0,1:T(8,128)(2,1)}), bf16[1024,3584]{0,1:T(8,128)(2,1)}) %reduce-scatter.8.cloned.1.call-update) | async-done | bytes 7340048 | tf_op jit(solution)/shard_map/reduce_scatter | solution.py:86
  414.8 9.6 %convert_multiply_fusion = f32[1024,3584]{0,1:T(8,128)} fusion(bf16[1024,3584]{0,1:T(8,128)(2,1)} %reduce-scatter.8.cloned.1.call-done, f32[3584]{0:T(1024)S(1)} %add_convert_fusion), kind=kLoop, calls=%fused_computation.3 | loop fusion | flops 7340032 | bytes 22034432 | tf_op jit(solution)/shard_map/mul | solution.py:38
  424.4 23.1 %convolution_multiply_fusion = f32[1024,28,128]{0,2,1:T(8,128)} fusion(f32[1024,28,128]{0,2,1:T(8,128)} %bitcast.27), kind=kOutput, calls=%fused_computation.5 | convolution fusion | flops 5641388032 | bytes 29360128 | tf_op jit(solution)/shard_map/rbi,ij->rbj/dot_general | solution.py:40
  447.5 14.3 %copy.31 = f32[1024,3584]{1,0:T(8,128)} copy(f32[1024,3584]{0,1:T(8,128)} %bitcast.26) | data formatting | bytes 29360128
  461.7 0.0 reduce-scatter.6.cloned.1.call-done
  (1 shorter events, 0.0 us)
Async XLA Ops:
  7.2 10.5 %copy-start.2 = (f32[16,3584]{1,0:T(8,128)S(1)}, f32[16,3584]{1,0:T(8,128)}, u32[]{:S(2)}) copy-start(f32[16,3584]{1,0:T(8,128)} %param.7) | copy-start | bytes 688132
  11.3 54.5 %all-to-all-start = ((bf16[128,4,2048]{0,2,1:T(8,128)(2,1)}), bf16[128,4,2048]{0,2,1:T(8,128)(2,1)S(1)}, u32[]{:S(2)}, u32[]{:S(2)}) async-start(bf16[128,4,2048]{0,2,1:T(8,128)(2,1)} %bitcast.30), calls=%async_computation | async-start | bytes 4194304 | tf_op jit(solution)/shard_map/all_to_all | solution.py:56
  17.6 137.8 %reduce-scatter.10.cloned.1.call-start = ((), (), s32[]{:S(2)}) async-start(), calls=%async_computation.7 | async-start | bytes 4587520
  81.6 6.2 %copy-start.1 = (bf16[128,3584]{1,0:T(8,128)(2,1)S(1)}, bf16[128,3584]{1,0:T(8,128)(2,1)}, u32[]{:S(2)}) copy-start(bf16[128,3584]{1,0:T(8,128)(2,1)} %param.8) | copy-start | bytes 2752516
  87.7 327.1 %reduce-scatter.8.cloned.1.call-start = ((), (), s32[]{:S(2)}) async-start(), calls=%async_computation.6 | async-start | bytes 22020096 | tf_op jit(solution)/shard_map/reduce_scatter | solution.py:86
  159.7 23.6 %collective-permute-start = (bf16[128,3584]{0,1:T(8,128)(2,1)S(1)}, bf16[128,3584]{0,1:T(8,128)(2,1)S(1)}, u32[]{:S(2)}, u32[]{:S(2)}) collective-permute-start(bf16[128,3584]{0,1:T(8,128)(2,1)S(1)} %get-tuple-element.15), channel_id=1, source_target_pairs={{0,8},{8,16},{16,24},{24,0},{1,9},{9,17},{17,25},{25,1},{2,10},{10... | collective-permute-start | bytes 2752520 | tf_op jit(solution)/shard_map/ppermute | solution.py:18
  183.3 22.8 %collective-permute-start.1 = (bf16[128,3584]{0,1:T(8,128)(2,1)S(1)}, bf16[128,3584]{0,1:T(8,128)(2,1)}, u32[]{:S(2)}, u32[]{:S(2)}) collective-permute-start(bf16[128,3584]{0,1:T(8,128)(2,1)S(1)} %collective-permute-done), channel_id=1, source_target_pairs={{0,8},{8,16},{16,24},{24,0},{1,9},{9,17},{17,25},{25,1},{2,10},{10... | collective-permute-start | bytes 2752520 | tf_op jit(solution)/shard_map/ppermute | solution.py:18
  206.1 22.1 %collective-permute-start.2 = (bf16[128,3584]{0,1:T(8,128)(2,1)}, bf16[128,3584]{0,1:T(8,128)(2,1)}, u32[]{:S(2)}, u32[]{:S(2)}) collective-permute-start(bf16[128,3584]{0,1:T(8,128)(2,1)} %collective-permute-done.1), channel_id=1, source_target_pairs={{0,8},{8,16},{16,24},{24,0},{1,9},{9,17},{17,25},{25,1},{2,10},{10... | collective-permute-start | bytes 2752520 | tf_op jit(solution)/shard_map/ppermute | solution.py:18
  206.1 32.3 %copy-start = (bf16[4,128,2048]{2,1,0:T(8,128)(2,1)S(1)}, bf16[4,128,2048]{2,1,0:T(8,128)(2,1)}, u32[]{:S(2)}) copy-start(bf16[4,128,2048]{2,1,0:T(8,128)(2,1)} %copy.26) | copy-start | bytes 6291460
  235.4 3.0 copy-start.3
  249.4 212.3 %reduce-scatter.6.cloned.1.call-start = ((), (), s32[]{:S(2)}) async-start(), calls=%async_computation.5 | async-start | bytes 2621440 | tf_op jit(solution)/shard_map/reduce_scatter | solution.py:80
  261.8 49.5 %copy-start.4 = (s32[3584]{0:T(1024)S(1)}, s32[3584]{0:T(1024)}, u32[]{:S(2)}) copy-start(s32[3584]{0:T(1024)} %param.9) | copy-start | bytes 43012
Sparse Core Ops, SparseCore 0:
  87.8 67.6 reduce-scatter.9
  249.6 165.2 reduce-scatter.7
  417.9 31.1 reduce-scatter.5
